TPU v7x, 256 devices: a whole 4x4x8 slice. The times are simulated.
256 devices in a mesh: dp: 32 (over z_lo, x, core), tensor: 8 (over y, z_hi).
Axes of the slice: x: 4, y: 4, z: 8 (z_hi: 2, z_lo: 4; z = z_hi * 4 + z_lo), core: 2. Of those that a mesh axis runs over, the one named last changes fastest.
Arguments:
- hidden: bfloat16 [32768, 28672], P('dp', 'tensor'), may hold values from -6 to 6
- out_grad: bfloat16 [32768, 8192], P('dp', 'tensor'), may hold values from -6 to 6
- proj_in: bfloat16 [28672, 64], P('tensor'), may hold values from -0.03125 to 0.03125
- proj_out: bfloat16 [8192, 64], P('tensor'), may hold values from -0.0625 to 0.0625
- owner_ids: int32 [32768, 1], P('dp'), may hold values from 0 to 31; in each aligned block of 1024 rows (0 to 1023, 1024 to 2047, ...) at most 128 rows name the same one
- example_ids: int32 [32768], P('dp'), may hold values from 0 to 127
Outputs:
- kernel: float32 [4096, 4096], P('tensor', 'dp')
Inputs may be any that keep to these rules, and one draw needn't show every extreme that they name: `owner_ids`: among the rows of one index of dp, at most 128 name the same owner, and every draw reaches 128.
All inputs are finite; a program needn't handle non-finite values.
Results may differ from a plain program's by a relative error of at most 0.009.
Values may be sent and summed in bfloat16 or wider, within the bound.
A program may use at most 64 MiB of HBM per device.

v0:
```python
import jax
import jax.numpy as jnp
from jax import lax
from jax.sharding import PartitionSpec as P

EX_DEV = 128


def outer_rows(x_rows, g_rows):
    return (x_rows[:, :, None] * g_rows[:, None, :]).reshape(
        x_rows.shape[0], x_rows.shape[1] * g_rows.shape[1]
    )


def member_dot(member, outer):
    member_half = member.astype(jnp.bfloat16)
    upper = outer.astype(jnp.bfloat16)
    lower = (outer - upper.astype(jnp.float32)).astype(jnp.bfloat16)
    first = jnp.dot(member_half, upper, preferred_element_type=jnp.float32)
    return first + jnp.dot(member_half, lower, preferred_element_type=jnp.float32)


def body(hidden, out_grad, proj_in, proj_out, owner_ids, example_ids):
    tensors = lax.axis_size("tensor")
    trank = lax.axis_index("tensor")
    groups = lax.axis_size("dp")
    width = proj_in.shape[1]
    share = width // tensors
    tok = hidden.shape[0]
    x_part = jnp.dot(hidden, proj_in, preferred_element_type=jnp.float32)
    g_part = jnp.dot(out_grad, proj_out, preferred_element_type=jnp.float32)
    send_rows = lax.psum(jnp.concatenate([x_part, g_part], 1), "tensor")
    x_start = trank * share
    columns = send_rows.shape[1]
    owners = owner_ids[:, 0]
    capacity = 4 * tok // groups
    owner_hot = (owners[:, None] == jnp.arange(groups, dtype=jnp.int32)[None, :]).astype(jnp.int32)
    slot_index = jnp.sum(jnp.cumsum(owner_hot, 0) * owner_hot, 1) - 1
    target = owners * capacity + slot_index
    row_buffer = jnp.zeros((groups * capacity, columns), jnp.float32).at[target].set(send_rows)
    id_buffer = (
        jnp.full((groups * capacity,), -1.0, jnp.float32)
        .at[target]
        .set(example_ids.astype(jnp.float32))
    )
    got_rows, got_ids = (
        lax.all_to_all(
            row_buffer.reshape(groups, capacity, columns),
            "dp",
            split_axis=0,
            concat_axis=0,
            tiled=True,
        ),
        lax.all_to_all(
            id_buffer.reshape(groups, capacity), "dp", split_axis=0, concat_axis=0, tiled=True
        ),
    )
    rows = got_rows.reshape(groups * capacity, columns)
    x_rows = lax.dynamic_slice_in_dim(rows, x_start, share, 1)
    g_rows = rows[:, columns - width :]
    member = (
        got_ids.reshape(1, groups * capacity) == jnp.arange(EX_DEV, dtype=jnp.float32)[:, None]
    ).astype(jnp.float32)
    sums = member_dot(member, outer_rows(x_rows, g_rows))
    counts = jnp.sum(member, 1)
    grads = (sums / jnp.maximum(counts, 1.0)[:, None]).astype(jnp.bfloat16)
    products = (
        lax.dot_general(
            lax.all_gather(grads, "dp", axis=0, tiled=True),
            grads,
            (((1,), (1,)), ((), ())),
            preferred_element_type=jnp.float32,
        )
        / width
    )
    return lax.psum_scatter(products, "tensor", scatter_dimension=0, tiled=True)


def solution(mesh):
    in_specs = (
        P("dp", "tensor"),
        P("dp", "tensor"),
        P("tensor", None),
        P("tensor", None),
        P("dp", None),
        P("dp"),
    )
    out_specs = P("tensor", "dp")
    return jax.shard_map(body, mesh=mesh, in_specs=in_specs, out_specs=out_specs, check_vma=False)
```

profile of v0, /device:TPU:6, one launch (start us, length us, event | category | flops | bytes accessed | tf_op | source)
XLA Modules:
  0.0 376.6 jit_solution(12380154530716794183)
XLA Ops:
  6.5 0.0 copy-start
  6.5 0.0 copy-start.2
  6.5 0.0 all-reduce.2.cloned.1.call-start
  6.5 5.6 %fusion.15 = f32[1024,64]{0,1:T(8,128)S(1)} fusion(bf16[1024,3584]{1,0:T(8,128)(2,1)} %param.6, bf16[3584,64]{0,1:T(8,128)(2,1)} %param.8), kind=kOutput, calls=%fused_computation.33 | convolution fusion | flops 469762048 | bytes 8060928 | tf_op jit(solution)/shard_map/dot_general | solution.py:30
  12.1 0.0 copy-done
  12.1 0.0 copy-done.2
  12.1 0.0 copy-start.3
  12.1 0.0 copy-start.4
  12.2 0.8 fusion.16
  12.9 0.9 pad_maximum_fusion
  13.8 0.0 all-reduce.2.cloned.1.call-update
  13.8 0.0 copy-done.3
  13.8 9.0 %reduce-window.6 = s32[32,8,128]{2,1,0:T(8,128)S(1)} reduce-window(s32[32,8,128]{2,1,0:T(8,128)S(1)} %fusion.12, s32[]{:T(128)} %constant.12.clone.1), window={size=1x1x128 pad=0_0x0_0x127_0}, to_apply=%region_0.0 | reduce-window | flops 4161536 | bytes 262148 | tf_op jit(solution)/shard_map/reduce-window
  22.8 0.1 slice.12
  22.9 0.1 copy.12
  23.1 0.1 copy.13
  23.2 0.1 broadcast_add_fusion
  23.3 0.0 copy-done.4
  23.4 4.9 %scatter_custom_fusion = f32[4096]{0:T(1024)} fusion(s32[1024]{0:T(1024)S(1)} %bitcast.45, f32[1024]{0:T(1024)S(1)} %convert_element_type.27, f32[]{:T(128)} %constant.10.clone.1), kind=kCustom, calls=%fused_computation.28 | custom fusion | bytes 16388 | tf_op jit(solution)/shard_map/scatter | solution.py:44
  28.3 9.0 %all-to-all-start = ((f32[32,1,128]{2,1,0:T(1,128)}), f32[32,1,128]{2,1,0:T(1,128)S(1)}, u32[]{:S(2)}, u32[]{:S(2)}) async-start(f32[32,1,128]{2,1,0:T(1,128)} %bitcast.6), calls=%async_computation | async-start | bytes 32768 | tf_op jit(solution)/shard_map/all_to_all | solution.py:54
  37.3 91.8 %all-reduce.2.cloned.1.call-done = f32[1024,128]{0,1:T(8,128)} async-done(((f32[1024,128]{0,1:T(8,128)}), f32[1024,128]{0,1:T(8,128)}) %all-reduce.2.cloned.1.call-update) | async-done | bytes 524304 | tf_op jit(solution)/shard_map/psum | solution.py:32
  129.1 1.2 copy.14
  130.3 4.5 %scatter_custom_fusion.1 = f32[4096,128]{1,0:T(8,128)} fusion(s32[1024]{0:T(1024)S(1)} %bitcast.46, f32[1024,128]{1,0:T(8,128)S(1)} %copy.14, f32[]{:T(128)} %constant.6.clone.1), kind=kCustom, calls=%fused_computation.15 | custom fusion | bytes 2097156 | tf_op jit(solution)/shard_map/scatter | solution.py:40
  134.8 0.0 all-to-all-done
  134.8 5.0 %all-to-all-start.1 = ((f32[32,128,128]{2,1,0:T(8,128)}), f32[32,128,128]{2,1,0:T(8,128)}, u32[]{:S(2)}, u32[]{:S(2)}) async-start(f32[32,128,128]{2,1,0:T(8,128)} %bitcast.36), calls=%async_computation.1 | async-start | bytes 4194304 | tf_op jit(solution)/shard_map/all_to_all | solution.py:47
  139.8 0.0 all-gather.2.cloned.1.call-start
  139.8 0.3 convert_reduce_fusion
  140.1 48.2 %all-to-all-done.1 = f32[32,128,128]{2,1,0:T(8,128)} async-done(((f32[32,128,128]{2,1,0:T(8,128)}), f32[32,128,128]{2,1,0:T(8,128)}, u32[]{:S(2)}, u32[]{:S(2)}) %all-to-all-start.1) | async-done | bytes 2097184 | tf_op jit(solution)/shard_map/all_to_all | solution.py:47
  188.3 3.5 slice.14
  191.8 3.5 constant_dynamic-slice_fusion
  195.3 2.2 copy.17
  197.5 2.2 copy.18
  199.7 1.0 broadcast_multiply_fusion
  200.7 4.7 %fusion = (bf16[4096,512]{0,1:T(8,128)(2,1)}, bf16[4096,512]{0,1:T(8,128)(2,1)}) fusion(f32[4096,8,64]{0,2,1:T(8,128)S(1)} %broadcast_multiply_fusion), kind=kLoop, calls=%fused_computation.4 | loop fusion | flops 8388608 | bytes 16777216 | tf_op jit(solution)/shard_map/convert_element_type | solution.py:18
  205.4 0.0 copy-start.1
  205.4 3.8 %fusion.1 = f32[128,512]{1,0:T(8,128)S(1)} fusion(bf16[4096,512]{0,1:T(8,128)(2,1)} %get-tuple-element.5, f32[4096]{0:T(1024)S(1)} %bitcast.39), kind=kOutput, calls=%fused_computation.10 | convolution fusion | flops 538443776 | bytes 4472832 | tf_op jit(solution)/shard_map/dot_general | solution.py:20
  209.3 0.0 copy-done.1
  209.3 2.2 fusion.5
  211.5 0.0 all-gather.2.cloned.1.call-update
  211.5 0.0 reduce-scatter.2.cloned.1.call-start
  211.5 58.5 %all-gather.2.cloned.1.call-done = bf16[4096,512]{1,0:T(8,128)(2,1)} async-done(((bf16[128,512]{1,0:T(8,128)(2,1)}), bf16[4096,512]{1,0:T(8,128)(2,1)}) %all-gather.2.cloned.1.call-update) | async-done | bytes 4194320 | tf_op jit(solution)/shard_map/all_gather | solution.py:69
  270.1 4.8 %convolution_multiply_fusion = f32[4096,128]{1,0:T(8,128)} fusion(bf16[4096,512]{1,0:T(8,128)(2,1)} %all-gather.2.cloned.1.call-done, bf16[128,512]{1,0:T(8,128)(2,1)} %fusion.5), kind=kOutput, calls=%fused_computation.5 | convolution fusion | flops 537395200 | bytes 6422528 | tf_op jit(solution)/shard_map/dot_general | solution.py:68
  274.8 0.0 reduce-scatter.2.cloned.1.call-update
  274.9 95.2 %reduce-scatter.2.cloned.1.call-done = f32[512,128]{1,0:T(8,128)} async-done(((f32[4096,128]{1,0:T(8,128)}), f32[512,128]{1,0:T(8,128)}) %reduce-scatter.2.cloned.1.call-update) | async-done | bytes 262160 | tf_op jit(solution)/shard_map/reduce_scatter | solution.py:76
  (8 shorter events, 0.1 us)
Async XLA Ops:
  6.5 5.6 %copy-start = (bf16[1024,1024]{1,0:T(8,128)(2,1)S(1)}, bf16[1024,1024]{1,0:T(8,128)(2,1)}, u32[]{:S(2)}) copy-start(bf16[1024,1024]{1,0:T(8,128)(2,1)} %param.7) | copy-start | bytes 6291460
  6.5 5.6 %copy-start.2 = (bf16[1024,64]{0,1:T(8,128)(2,1)S(1)}, bf16[1024,64]{0,1:T(8,128)(2,1)}, u32[]{:S(2)}) copy-start(bf16[1024,64]{0,1:T(8,128)(2,1)} %param.9) | copy-start | bytes 393220
  6.5 122.5 %all-reduce.2.cloned.1.call-start = ((), (), s32[]{:S(2)}) async-start(), calls=%async_computation.3 | async-start | bytes 1048576 | tf_op jit(solution)/shard_map/psum | solution.py:32
  12.1 1.7 copy-start.3
  12.1 11.2 %copy-start.4 = (s32[1024]{0:T(1024)S(1)}, s32[1024]{0:T(1024)}, u32[]{:S(2)}) copy-start(s32[1024]{0:T(1024)} %param.11) | copy-start | bytes 12292
  28.3 106.5 %all-to-all-start = ((f32[32,1,128]{2,1,0:T(1,128)}), f32[32,1,128]{2,1,0:T(1,128)S(1)}, u32[]{:S(2)}, u32[]{:S(2)}) async-start(f32[32,1,128]{2,1,0:T(1,128)} %bitcast.6), calls=%async_computation | async-start | bytes 32768 | tf_op jit(solution)/shard_map/all_to_all | solution.py:54
  134.8 53.5 %all-to-all-start.1 = ((f32[32,128,128]{2,1,0:T(8,128)}), f32[32,128,128]{2,1,0:T(8,128)}, u32[]{:S(2)}, u32[]{:S(2)}) async-start(f32[32,128,128]{2,1,0:T(8,128)} %bitcast.36), calls=%async_computation.1 | async-start | bytes 4194304 | tf_op jit(solution)/shard_map/all_to_all | solution.py:47
  139.8 130.3 %all-gather.2.cloned.1.call-start = ((), (), s32[]{:S(2)}) async-start(), calls=%async_computation.4 | async-start | bytes 4325376 | tf_op jit(solution)/shard_map/all_gather | solution.py:69
  205.4 3.9 %copy-start.1 = (bf16[4096,512]{0,1:T(8,128)(2,1)S(1)}, bf16[4096,512]{0,1:T(8,128)(2,1)}, u32[]{:S(2)}) copy-start(bf16[4096,512]{0,1:T(8,128)(2,1)} %get-tuple-element.6) | copy-start | bytes 12582916
  211.5 158.6 %reduce-scatter.2.cloned.1.call-start = ((), (), s32[]{:S(2)}) async-start(), calls=%async_computation.5 | async-start | bytes 2359296 | tf_op jit(solution)/shard_map/reduce_scatter | solution.py:76
Sparse Core Ops, SparseCore 0:
  13.9 115.0 all-reduce.1
  211.6 58.4 all-gather.1
  275.0 95.0 reduce-scatter.1
where the time goes:
time: 377 us
  waiting for transfers between devices  294 us (78%)
  local copies, waits for them, and re-layouts  22.3 us (6%)
  matrix products  17.1 us (5%)
  other arithmetic  16.1 us (4%)
  starting transfers between devices  14.1 us (4%)
  between operations  13.3 us (4%)
    reduce_scatter x1, waiting for transfers between devices, body(): return lax.psum_scatter(products, 'tensor', scatter_dimension=0, tiled=True)  95.2 us
    psum x1, waiting for transfers between devices, body(): send_rows = lax.psum(jnp.concatenate([x_part, g_part], 1), 'tensor')  91.8 us
    all_gather x1, waiting for transfers between devices, body(): lax.all_gather(grads, 'dp', axis=0, tiled=True)  58.5 us
    all_to_all x1, waiting for transfers between devices, body(): lax.all_to_all(row_buffer.reshape(groups, capacity, columns), 'dp', split...  48.2 us
    another operation x3, other arithmetic  9.15 us
    all_to_all x1, starting transfers between devices, body(): lax.all_to_all(id_buffer.reshape(groups, capacity), 'dp', split_axis=0, c...  8.99 us
  transfers between devices with their start and end apart: 5, of which 4 were waited for; matrix products, arithmetic and copies ran while one was open for 5% of the time, Pallas kernels for 0%

commit v1 on v0

--- a/solution.py
+++ b/solution.py
@@ -29,7 +29,8 @@
     tok = hidden.shape[0]
     x_part = jnp.dot(hidden, proj_in, preferred_element_type=jnp.float32)
     g_part = jnp.dot(out_grad, proj_out, preferred_element_type=jnp.float32)
-    send_rows = lax.psum(jnp.concatenate([x_part, g_part], 1), "tensor")
+    values = jnp.concatenate([x_part, g_part], 1)
+    send_rows = jnp.sum(lax.all_gather(values, "tensor"), axis=0)
     x_start = trank * share
     columns = send_rows.shape[1]
     owners = owner_ids[:, 0]

time: 377 us -> 377 us (level)
  waiting for transfers between devices: 294 us -> 288 us
  local copies, waits for them, and re-layouts: 22.3 us -> 26.7 us
    psum x1 -> x0, waiting for transfers between devices: 91.8 us -> none  [body(): send_rows = lax.psum(jnp.concatenate([x_part, g_part], 1), 'tensor')]
    all_gather x0 -> x1, waiting for transfers between devices: none -> 86.7 us  [body(): send_rows = jnp.sum(lax.all_gather(values, 'tensor'), axis=0)]
    unnamed x12 -> x13, local copies, waits for them, and re-layouts: 4.36 us -> 9.8 us
  transfers between devices with their start and end apart: 5 -> 5, of which waited for: 4 -> 4; matrix products, arithmetic and copies ran while one was open for 5% -> 7% of each run, Pallas kernels for 0% -> 0%
where the time goes in v1:
time: 377 us
  waiting for transfers between devices  288 us (76%)
  local copies, waits for them, and re-layouts  26.7 us (7%)
  matrix products  17.1 us (5%)
  other arithmetic  17.1 us (5%)
  starting transfers between devices  14.3 us (4%)
  between operations  13.3 us (4%)
    reduce_scatter x1, waiting for transfers between devices, body(): return lax.psum_scatter(products, 'tensor', scatter_dimension=0, tiled=True)  95.4 us
    all_gather x1, waiting for transfers between devices, body(): send_rows = jnp.sum(lax.all_gather(values, 'tensor'), axis=0)  86.7 us
    all_gather x1, waiting for transfers between devices, body(): lax.all_gather(grads, 'dp', axis=0, tiled=True)  58.1 us
    all_to_all x1, waiting for transfers between devices, body(): lax.all_to_all(row_buffer.reshape(groups, capacity, columns), 'dp', split...  48 us
    unnamed x13, local copies, waits for them, and re-layouts  9.8 us
    another operation x3, other arithmetic  9.15 us
    all_to_all x1, starting transfers between devices, body(): lax.all_to_all(id_buffer.reshape(groups, capacity), 'dp', split_axis=0, c...  9 us
  transfers between devices with their start and end apart: 5, of which 4 were waited for; matrix products, arithmetic and copies ran while one was open for 7% of the time, Pallas kernels for 0%

profile of v1, /device:TPU:6, one launch (start us, length us, event | category | flops | bytes accessed | tf_op | source)
XLA Modules:
  0.0 376.7 jit_solution(4223373167693843852)
XLA Ops:
  6.5 0.0 copy-start
  6.5 0.0 copy-start.2
  6.5 0.0 copy-start.3
  6.5 0.0 all-gather.6.cloned.1.call-start
  6.5 5.6 %fusion.15 = f32[1024,64]{0,1:T(8,128)S(1)} fusion(bf16[1024,3584]{1,0:T(8,128)(2,1)} %param.6, bf16[3584,64]{0,1:T(8,128)(2,1)} %param.8), kind=kOutput, calls=%fused_computation.34 | convolution fusion | flops 469762048 | bytes 8060928 | tf_op jit(solution)/shard_map/dot_general | solution.py:30
  12.1 0.0 copy-done
  12.1 0.0 copy-done.2
  12.1 0.0 copy-start.4
  12.1 0.8 fusion.16
  12.9 0.8 pad_maximum_fusion
  13.7 0.0 all-gather.6.cloned.1.call-update
  13.8 0.0 copy-done.3
  13.8 9.0 %reduce-window.6 = s32[32,8,128]{2,1,0:T(8,128)S(1)} reduce-window(s32[32,8,128]{2,1,0:T(8,128)S(1)} %fusion.12, s32[]{:T(128)} %constant.12.clone.1), window={size=1x1x128 pad=0_0x0_0x127_0}, to_apply=%region_0.0 | reduce-window | flops 4161536 | bytes 262148 | tf_op jit(solution)/shard_map/reduce-window
  22.8 0.1 slice.12
  22.9 0.1 copy.18
  23.1 0.1 copy.19
  23.2 0.0 copy-done.4
  23.2 0.1 broadcast_add_fusion
  23.3 4.9 %scatter_custom_fusion = f32[4096]{0:T(1024)} fusion(s32[1024]{0:T(1024)S(1)} %bitcast.51, f32[1024]{0:T(1024)S(1)} %convert_element_type.27, f32[]{:T(128)} %constant.10.clone.1), kind=kCustom, calls=%fused_computation.29 | custom fusion | bytes 16388 | tf_op jit(solution)/shard_map/scatter | solution.py:45
  28.2 9.0 %all-to-all-start = ((f32[32,1,128]{2,1,0:T(1,128)}), f32[32,1,128]{2,1,0:T(1,128)S(1)}, u32[]{:S(2)}, u32[]{:S(2)}) async-start(f32[32,1,128]{2,1,0:T(1,128)} %bitcast.6), calls=%async_computation | async-start | bytes 32768 | tf_op jit(solution)/shard_map/all_to_all | solution.py:55
  37.2 86.7 %all-gather.6.cloned.1.call-done = f32[8192,128]{0,1:T(8,128)} async-done(((f32[1024,128]{0,1:T(8,128)}), f32[8192,128]{0,1:T(8,128)}) %all-gather.6.cloned.1.call-update) | async-done | bytes 4194320 | tf_op jit(solution)/shard_map/all_gather | solution.py:33
  124.0 5.4 %copy.26 = f32[16,8,8,1024]{3,2,1,0:T(8,128)S(1)} copy(f32[16,8,8,1024]{3,1,2,0:T(8,128)} %bitcast.42) | data formatting | bytes 8388608
  129.4 1.0 bitcast_reduce_fusion
  130.4 0.2 copy.20
  130.6 4.5 %scatter_custom_fusion.1 = f32[4096,128]{1,0:T(8,128)} fusion(s32[1024]{0:T(1024)S(1)} %bitcast.52, f32[1024,128]{1,0:T(8,128)S(1)} %copy.20, f32[]{:T(128)} %constant.6.clone.1), kind=kCustom, calls=%fused_computation.16 | custom fusion | bytes 2097156 | tf_op jit(solution)/shard_map/scatter | solution.py:41
  135.1 0.0 all-to-all-done
  135.1 5.0 %all-to-all-start.1 = ((f32[32,128,128]{2,1,0:T(8,128)}), f32[32,128,128]{2,1,0:T(8,128)}, u32[]{:S(2)}, u32[]{:S(2)}) async-start(f32[32,128,128]{2,1,0:T(8,128)} %bitcast.41), calls=%async_computation.1 | async-start | bytes 4194304 | tf_op jit(solution)/shard_map/all_to_all | solution.py:48
  140.1 0.2 all-gather.4.cloned.1.call-start
  140.4 0.3 convert_reduce_fusion
  140.7 48.0 %all-to-all-done.1 = f32[32,128,128]{2,1,0:T(8,128)} async-done(((f32[32,128,128]{2,1,0:T(8,128)}), f32[32,128,128]{2,1,0:T(8,128)}, u32[]{:S(2)}, u32[]{:S(2)}) %all-to-all-start.1) | async-done | bytes 2097184 | tf_op jit(solution)/shard_map/all_to_all | solution.py:48
  188.6 3.5 slice.14
  192.1 3.5 constant_dynamic-slice_fusion
  195.7 2.2 copy.23
  197.8 2.2 copy.24
  200.0 1.0 broadcast_multiply_fusion
  201.0 4.7 %fusion = (bf16[4096,512]{0,1:T(8,128)(2,1)}, bf16[4096,512]{0,1:T(8,128)(2,1)}) fusion(f32[4096,8,64]{0,2,1:T(8,128)S(1)} %broadcast_multiply_fusion), kind=kLoop, calls=%fused_computation.4 | loop fusion | flops 8388608 | bytes 16777216 | tf_op jit(solution)/shard_map/convert_element_type | solution.py:18
  205.8 0.0 copy-start.1
  205.8 3.8 %fusion.1 = f32[128,512]{1,0:T(8,128)S(1)} fusion(bf16[4096,512]{0,1:T(8,128)(2,1)} %get-tuple-element.5, f32[4096]{0:T(1024)S(1)} %bitcast.45), kind=kOutput, calls=%fused_computation.11 | convolution fusion | flops 538443776 | bytes 4472832 | tf_op jit(solution)/shard_map/dot_general | solution.py:20
  209.6 0.0 copy-done.1
  209.6 2.2 fusion.5
  211.8 0.0 all-gather.4.cloned.1.call-update
  211.8 0.0 reduce-scatter.2.cloned.1.call-start
  211.9 58.1 %all-gather.4.cloned.1.call-done = bf16[4096,512]{1,0:T(8,128)(2,1)} async-done(((bf16[128,512]{1,0:T(8,128)(2,1)}), bf16[4096,512]{1,0:T(8,128)(2,1)}) %all-gather.4.cloned.1.call-update) | async-done | bytes 4194320 | tf_op jit(solution)/shard_map/all_gather | solution.py:70
  270.0 4.8 %convolution_multiply_fusion = f32[4096,128]{1,0:T(8,128)} fusion(bf16[4096,512]{1,0:T(8,128)(2,1)} %all-gather.4.cloned.1.call-done, bf16[128,512]{1,0:T(8,128)(2,1)} %fusion.5), kind=kOutput, calls=%fused_computation.5 | convolution fusion | flops 537395200 | bytes 6422528 | tf_op jit(solution)/shard_map/dot_general | solution.py:69
  274.8 0.0 reduce-scatter.2.cloned.1.call-update
  274.8 95.4 %reduce-scatter.2.cloned.1.call-done = f32[512,128]{1,0:T(8,128)} async-done(((f32[4096,128]{1,0:T(8,128)}), f32[512,128]{1,0:T(8,128)}) %reduce-scatter.2.cloned.1.call-update) | async-done | bytes 262160 | tf_op jit(solution)/shard_map/reduce_scatter | solution.py:77
  (8 shorter events, 0.1 us)
Async XLA Ops:
  6.5 5.6 %copy-start = (bf16[1024,1024]{1,0:T(8,128)(2,1)S(1)}, bf16[1024,1024]{1,0:T(8,128)(2,1)}, u32[]{:S(2)}) copy-start(bf16[1024,1024]{1,0:T(8,128)(2,1)} %param.7) | copy-start | bytes 6291460
  6.5 5.6 %copy-start.2 = (bf16[1024,64]{0,1:T(8,128)(2,1)S(1)}, bf16[1024,64]{0,1:T(8,128)(2,1)}, u32[]{:S(2)}) copy-start(bf16[1024,64]{0,1:T(8,128)(2,1)} %param.9) | copy-start | bytes 393220
  6.5 7.2 %copy-start.3 = (s32[1024,1]{0,1:T(1,128)S(1)}, s32[1024,1]{0,1:T(1,128)}, u32[]{:S(2)}) copy-start(s32[1024,1]{0,1:T(1,128)} %param.10) | copy-start | bytes 12292
  6.5 117.4 %all-gather.6.cloned.1.call-start = ((), (), s32[]{:S(2)}) async-start(), calls=%async_computation.5 | async-start | bytes 4718592 | tf_op jit(solution)/shard_map/all_gather | solution.py:33
  12.1 11.0 %copy-start.4 = (s32[1024]{0:T(1024)S(1)}, s32[1024]{0:T(1024)}, u32[]{:S(2)}) copy-start(s32[1024]{0:T(1024)} %param.11) | copy-start | bytes 12292
  28.2 106.9 %all-to-all-start = ((f32[32,1,128]{2,1,0:T(1,128)}), f32[32,1,128]{2,1,0:T(1,128)S(1)}, u32[]{:S(2)}, u32[]{:S(2)}) async-start(f32[32,1,128]{2,1,0:T(1,128)} %bitcast.6), calls=%async_computation | async-start | bytes 32768 | tf_op jit(solution)/shard_map/all_to_all | solution.py:55
  135.1 53.5 %all-to-all-start.1 = ((f32[32,128,128]{2,1,0:T(8,128)}), f32[32,128,128]{2,1,0:T(8,128)}, u32[]{:S(2)}, u32[]{:S(2)}) async-start(f32[32,128,128]{2,1,0:T(8,128)} %bitcast.41), calls=%async_computation.1 | async-start | bytes 4194304 | tf_op jit(solution)/shard_map/all_to_all | solution.py:48
  140.1 129.9 %all-gather.4.cloned.1.call-start = ((), (), s32[]{:S(2)}) async-start(), calls=%async_computation.3 | async-start | bytes 4325376 | tf_op jit(solution)/shard_map/all_gather | solution.py:70
  205.8 3.9 %copy-start.1 = (bf16[4096,512]{0,1:T(8,128)(2,1)S(1)}, bf16[4096,512]{0,1:T(8,128)(2,1)}, u32[]{:S(2)}) copy-start(bf16[4096,512]{0,1:T(8,128)(2,1)} %get-tuple-element.6) | copy-start | bytes 12582916
  211.8 158.3 %reduce-scatter.2.cloned.1.call-start = ((), (), s32[]{:S(2)}) async-start(), calls=%async_computation.4 | async-start | bytes 2359296 | tf_op jit(solution)/shard_map/reduce_scatter | solution.py:77
Sparse Core Ops, SparseCore 0:
  13.9 110.0 all-gather.5
  212.0 58.0 all-gather.3
  274.9 95.1 reduce-scatter.1
